TPU v7x, 32 devices: a whole 2x2x4 slice. The times are simulated.
32 devices in a mesh: tok: 2 (over core), head: 4 (over y, x), exp: 4 (over z).
Axes of the slice: x: 2, y: 2, z: 4, core: 2. Of those that a mesh axis runs over, the one named last changes fastest.
Arguments:
- context: bfloat16 [4, 64, 4096], P('exp', 'tok', 'head'), may hold values from -6 to 6
- out_proj: bfloat16 [4096, 4096], P('head', 'exp'), may hold values from -0.125 to 0.125
- stream: float32 [4, 64, 4096], P('exp', 'tok', 'head'), may hold values from -75 to 75
- norm_gain: float32 [4096], replicated, may hold values from 0.1 to 1.9
- expert_ids: int32 [4, 64, 8], P('exp', 'tok'), may hold values from 0 to 31, as said below
- slot_ids: int32 [4, 64, 8], P('exp', 'tok'), may hold values from -1 to 11, as said below
- gate_probs: float32 [4, 64, 8], P('exp', 'tok'), may hold values from 0.02 to 0.3
- w_gate: bfloat16 [32, 3072, 4096], P(('tok', 'exp'), 'head'), may hold values from -0.09375 to 0.09375
- w_up: bfloat16 [32, 3072, 4096], P(('tok', 'exp'), 'head'), may hold values from -0.09375 to 0.09375
- w_down: bfloat16 [32, 3072, 4096], P(('tok', 'exp'), 'head'), may hold values from -0.15625 to 0.15625
Outputs:
- mixed: float32 [4, 64, 4096], P('exp', 'tok', 'head')
Inputs may be any that keep to these rules, and one draw needn't show every extreme that they name: `expert_ids`: each token names 8 different experts. `slot_ids`: within a block of 32 consecutive tokens of one image, the choices of one expert take slots 0, 1, 2, ... in token order until its 12 slots are full, later ones get -1; in every block some expert fills all 12 slots.
All inputs are finite; a program needn't handle non-finite values.
Results may differ from a plain program's by a relative error of at most 0.0034.
Values may be sent and summed in bfloat16 or wider, within the bound.
A program may use at most 128 MiB of HBM per device.

v0:
```python
import functools

import jax
import jax.numpy as jnp
from jax import lax
from jax.experimental import pallas as pl
from jax.experimental.pallas import tpu as pltpu
from jax.sharding import PartitionSpec as P

MESH = pl.DeviceIdType.MESH
LANES = 128
SLOT_BYTES = 50_400_000
F32 = jnp.float32
BF16 = jnp.bfloat16
eps_value = 1e-05


def kernel(
    n_tok, n_head, n_exp, n_slots,
    ctx_ref, proj_hbm, stream_ref, gain_ref, ids_ref, slots_ref, probs_ref,
    wg_hbm, wu_hbm, wd_hbm,
    out_ref,
    proj, wbuf, ctx_all, wall, stream_bf, stream_t, pbf, pown, prs,
    attn_buf, attn_in, ssq, x, hid, acc, obf, tin, hsend, hrecv, zsend, zrecv,
    proj_sem, w_sem, ctx_s, ctx_r, wz_s, wz_r, wt_s, wt_r, st_s, st_r,
    prs_s, prs_r, at_s, at_r, xz_s, xz_r, qz_s, qz_r, xh_s, xh_r, qh_s, qh_r,
    xt_s, xt_r, qt_s, qt_r, to_s, to_r, ho_s, ho_r, zo_s, zo_r,
):
    t, h, e = lax.axis_index("tok"), lax.axis_index("head"), lax.axis_index("exp")
    rows, width = stream_ref.shape
    n_local, n_hid, model = wg_hbm.shape
    tokens = n_tok * n_exp * rows
    tp = 1 - t
    turned = {"tok": t, "head": e, "exp": h}
    mine = h == e

    def send(src, dst, s_sem, r_sem, device):
        return pltpu.make_async_remote_copy(
            src_ref=src, dst_ref=dst, send_sem=s_sem, recv_sem=r_sem,
            device_id=device, device_id_type=MESH,
        )

    def on_exp(k):
        return {"exp": lax.rem(e + k, n_exp)}

    def on_head(k):
        return {"head": lax.rem(h + k, n_head)}

    on_tok = {"tok": tp}

    sources = [s.at[j] for j in range(n_local) for s in (wg_hbm, wu_hbm)]
    sources += [wd_hbm.at[j] for j in range(n_local)]

    def w_copy(q):
        return pltpu.make_async_copy(sources[q], wbuf.at[q % n_slots], w_sem.at[q % n_slots])

    proj_copy = pltpu.make_async_copy(proj_hbm, proj, proj_sem)
    proj_copy.start()

    barrier = pltpu.get_barrier_semaphore()
    for k in range(1, n_exp):
        pl.semaphore_signal(barrier, inc=1, device_id=on_exp(k), device_id_type=MESH)
    for k in range(1, n_head):
        pl.semaphore_signal(barrier, inc=1, device_id=on_head(k), device_id_type=MESH)
    pl.semaphore_signal(barrier, inc=1, device_id=on_tok, device_id_type=MESH)

    @pl.when(jnp.logical_not(mine))
    def _():
        pl.semaphore_signal(barrier, inc=1, device_id=turned, device_id_type=MESH)

    stream_bf[...] = stream_ref[...].astype(BF16)
    lane = lax.broadcasted_iota(jnp.int32, (rows, LANES), 1)
    n_experts = wall.shape[2]
    expert_row = lax.broadcasted_iota(jnp.int32, (n_experts, rows), 0)
    dense = jnp.zeros((n_experts, rows), F32)
    for k in range(ids_ref.shape[0]):
        hit = (ids_ref[k : k + 1, :] == expert_row) & (slots_ref[k : k + 1, :] >= 0)
        dense = dense + jnp.where(hit, probs_ref[k : k + 1, :], 0.0)
    wall[0, e] = jnp.zeros((n_experts, LANES), F32)
    wall[0, e, :, :rows] = dense
    ctx_all[e] = ctx_ref[...]

    @pl.when(mine)
    def _():
        pl.semaphore_wait(barrier, n_exp - 1 + n_head - 1 + 1)

    @pl.when(jnp.logical_not(mine))
    def _():
        pl.semaphore_wait(barrier, n_exp - 1 + n_head - 1 + 2)

    ctx_c = [
        send(ctx_ref, ctx_all.at[e], ctx_s.at[k], ctx_r.at[k], on_exp(k)) for k in range(1, n_exp)
    ]
    for c in ctx_c:
        c.start()
    stream_c = send(stream_bf, stream_t, st_s, st_r, turned)

    @pl.when(jnp.logical_not(mine))
    def _():
        stream_c.start()

    wz_c = [
        send(wall.at[0, e], wall.at[0, e], wz_s.at[k], wz_r.at[k], on_exp(k))
        for k in range(1, n_exp)
    ]
    for c in wz_c:
        c.start()
    proj_copy.wait()
    for c in ctx_c:
        c.wait()

    tile = min(width, 256)

    def project(i, carry):
        cols = pl.ds(pl.multiple_of(i * tile, tile), tile)
        part = jnp.dot(
            ctx_all[...].reshape(n_exp * rows, ctx_ref.shape[1]), proj[:, cols],
            preferred_element_type=F32,
        ).reshape(n_exp, rows, tile)
        pown[:, :, cols] = part
        pbf[:, :, cols] = part.astype(BF16)
        return carry

    lax.fori_loop(0, proj.shape[1] // tile, project, 0)
    prs_c = [
        send(
            pbf.at[lax.rem(h + k, n_head)], prs.at[k - 1], prs_s.at[k], prs_r.at[k], on_head(k)
        )
        for k in range(1, n_head)
    ]
    for c in prs_c:
        c.start()
    for q in range(n_slots):
        w_copy(q).start()
    for c in wz_c:
        c.wait()
    wt_c = send(wall.at[0], wall.at[1], wt_s, wt_r, on_tok)
    wt_c.start()

    @pl.when(jnp.logical_not(mine))
    def _():
        stream_c.wait()

    @pl.when(mine)
    def _():
        stream_t[...] = stream_bf[...]

    for c in prs_c:
        c.wait()
    attn = pown[h]
    for k in range(1, n_head):
        attn = attn + prs[k - 1].astype(F32)
    attn_buf[...] = attn
    attn_c = send(attn_buf, attn_in, at_s, at_r, turned)

    resid = attn + stream_t[...].astype(F32)
    gain = gain_ref[:, pl.ds(pl.multiple_of(e * width, LANES), width)]
    own_cols = pl.ds(pl.multiple_of(e * width, LANES), width)
    x[0, h, :, own_cols] = (resid * gain).astype(BF16)
    square = jnp.sum(resid * resid, axis=1, keepdims=True)
    row_id = lax.broadcasted_iota(jnp.int32, (rows, LANES), 0)
    flat = jnp.sum(jnp.where(row_id == lane, square, 0.0), axis=0, keepdims=True)
    ssq[0, h, e] = jnp.broadcast_to(flat, (8, LANES))

    def x_at(i, c):
        return x.at[0, i, :, pl.ds(pl.multiple_of(c * width, LANES), width)]

    xz_c = [
        send(x_at(h, e), x_at(h, e), xz_s.at[k], xz_r.at[k], on_exp(k)) for k in range(1, n_exp)
    ]
    qz_c = [
        send(ssq.at[0, h, e], ssq.at[0, h, e], qz_s.at[k], qz_r.at[k], on_exp(k))
        for k in range(1, n_exp)
    ]
    for a, b in zip(xz_c, qz_c):
        a.start()
        b.start()
    xh_c = []
    for j in range(n_exp):
        if j:
            xz_c[j - 1].wait_recv()
        piece = lax.rem(e - j + n_exp, n_exp)
        for k in range(1, n_head):
            c = send(x_at(h, piece), x_at(h, piece), xh_s.at[k, j], xh_r.at[k, j], on_head(k))
            c.start()
            xh_c.append((k, j, c))
    for c in qz_c:
        c.wait_recv()
    qh_c = [
        send(ssq.at[0, h], ssq.at[0, h], qh_s.at[k], qh_r.at[k], on_head(k))
        for k in range(1, n_head)
    ]
    for c in qh_c:
        c.start()

    @pl.when(jnp.logical_not(mine))
    def _():
        attn_c.start()

    xt_c = []
    for k in range(n_head):
        if k:
            for kk, j, c in xh_c:
                if kk == k:
                    c.wait_recv()
            qh_c[k - 1].wait_recv()
        image = lax.rem(h - k + n_head, n_head)
        a = send(x.at[0, image], x.at[1, image], xt_s.at[k], xt_r.at[k], on_tok)
        b = send(ssq.at[0, image], ssq.at[1, image], qt_s.at[k], qt_r.at[k], on_tok)
        a.start()
        b.start()
        xt_c += [a, b]
    for c in xt_c:
        c.wait_recv()
    wt_c.wait()

    token_row = lax.rem(lax.broadcasted_iota(jnp.int32, (tokens, LANES), 0), rows)
    token_lane = lax.broadcasted_iota(jnp.int32, (tokens, LANES), 1)

    def column(value):
        wide = jnp.broadcast_to(value, (n_tok, n_exp, rows, LANES)).reshape(tokens, LANES)
        return jnp.sum(jnp.where(token_row == token_lane, wide, 0.0), axis=1, keepdims=True)

    sums = column(jnp.sum(ssq[...], axis=2)[:, :, 0:1, :])
    scale = lax.rsqrt(sums / model + eps_value)
    expert_of = lax.broadcasted_iota(jnp.int32, wall.shape, 2)

    hid_tile = 256 if n_hid % 256 == 0 else n_hid
    col_tile = min(width, 512)
    per = width // col_tile

    n_tiles = n_hid // hid_tile
    for j in range(n_local):
        for m in range(2):
            w_copy(2 * j + m).wait()
        gs, us = (2 * j) % n_slots, (2 * j + 1) % n_slots
        number = (t * n_exp + e) * n_local + j
        picked = jnp.where(expert_of == number, wall[...], 0.0)
        gate_w = column(jnp.sum(picked, axis=2, keepdims=True))

        def up(i, carry):
            span = pl.ds(pl.multiple_of(i * hid_tile, hid_tile), hid_tile)
            dims = (((1,), (1,)), ((), ()))
            xv = x[...].reshape(tokens, model)
            g = lax.dot_general(xv, wbuf[gs, span, :], dims, preferred_element_type=F32) * scale
            u = lax.dot_general(xv, wbuf[us, span, :], dims, preferred_element_type=F32) * scale
            value = g / (1.0 + jnp.exp(-g)) * u * gate_w
            hid[j * n_tiles + i] = value.astype(BF16)
            return carry

        lax.fori_loop(0, n_tiles, up, 0)
        for m in range(2):
            if 2 * j + m + n_slots < 3 * n_local:
                w_copy(2 * j + m + n_slots).start()

    for j in range(n_local):
        w_copy(2 * n_local + j).wait()
    ho_c = []
    to_c = []

    def head_step(k):
        to_c[k].wait_recv()
        if k < n_head - 1:
            hsend[k] = (acc[k] + tin[k].astype(F32)).astype(BF16)
            c = send(hsend.at[k], hrecv.at[k], ho_s.at[k], ho_r.at[k], on_head(k + 1))
            c.start()
            ho_c.append(c)

    for k in range(n_head):
        chunk = lax.rem(h + 1 + k, n_head)

        def step(i, carry):
            part = pl.ds(pl.multiple_of(i * col_tile, col_tile), col_tile)
            cols = pl.ds(pl.multiple_of(chunk * width + i * col_tile, col_tile), col_tile)
            value = jnp.zeros((tokens, col_tile), F32)
            for j in range(n_local):
                for i in range(n_tiles):
                    value = value + jnp.dot(
                        hid[j * n_tiles + i],
                        wbuf[
                            (2 * n_local + j) % n_slots, i * hid_tile : (i + 1) * hid_tile, cols
                        ],
                        preferred_element_type=F32,
                    )
            value = value.reshape(n_tok, n_exp, rows, col_tile)
            acc[k, :, :, part] = value[0]
            obf[k, :, :, part] = value[1].astype(BF16)
            return carry

        lax.fori_loop(0, per, step, 0)
        c = send(obf.at[k], tin.at[k], to_s.at[k], to_r.at[k], on_tok)
        c.start()
        to_c.append(c)
        if k:
            head_step(k - 1)
    head_step(n_head - 1)

    for c in ho_c:
        c.wait_recv()


    def mixed(image):
        value = acc[n_head - 1, image] + tin[n_head - 1, image].astype(F32)
        for k in range(n_head - 1):
            value = value + hrecv[k, image].astype(F32)
        return value

    zo_c = []
    for k in range(1, n_exp):
        zsend[k - 1] = mixed(lax.rem(e + k, n_exp)).astype(BF16)
        c = send(zsend.at[k - 1], zrecv.at[k - 1], zo_s.at[k], zo_r.at[k], on_exp(k))
        c.start()
        zo_c.append(c)

    @pl.when(jnp.logical_not(mine))
    def _():
        attn_c.wait()

    @pl.when(mine)
    def _():
        attn_in[...] = attn_buf[...]

    value = mixed(e) + attn_in[...]
    for k in range(1, n_exp):
        zo_c[k - 1].wait_recv()
        value = value + zrecv[k - 1].astype(F32)
    out_ref[...] = value
    for c in xz_c + qz_c + [c for _, _, c in xh_c] + qh_c + xt_c + to_c + ho_c + zo_c:
        c.wait_send()


def solution(mesh):
    n_tok, n_head, n_exp = mesh.shape["tok"], mesh.shape["head"], mesh.shape["exp"]

    def on_device(
        context, out_proj, stream, norm_gain, expert_ids, slot_ids, gate_probs, w_gate, w_up, w_down
    ):
        rows, width = stream.shape[1:]
        n_local, n_hid, model = w_gate.shape
        n_slots = min(3 * n_local, SLOT_BYTES // (n_hid * model * 2))
        tokens = n_tok * n_exp * rows
        hid_tile = 256 if n_hid % 256 == 0 else n_hid
        vmem = pl.BlockSpec(memory_space=pltpu.VMEM)
        hbm = pl.BlockSpec(memory_space=pl.ANY)
        dma = pltpu.SemaphoreType.DMA
        V = pltpu.VMEM
        scratch = [
            V(out_proj.shape, BF16),
            V((n_slots, n_hid, model), BF16),
            V((n_exp, rows, context.shape[2]), BF16),
            V((n_tok, n_exp, n_tok * n_exp * n_local, LANES), F32),
            V((rows, width), BF16),
            V((rows, width), BF16),
            V((n_exp, rows, width), BF16),
            V((n_exp, rows, width), F32),
            V((n_head - 1, rows, width), BF16),
            V((rows, width), F32),
            V((rows, width), F32),
            V((n_tok, n_exp, n_exp, 8, LANES), F32),
            V((n_tok, n_exp, rows, model), BF16),
            V((n_local * (n_hid // hid_tile), tokens, hid_tile), BF16),
            V((n_head, n_exp, rows, width), F32),
            V((n_head, n_exp, rows, width), BF16),
            V((n_head, n_exp, rows, width), BF16),
            V((n_head - 1, n_exp, rows, width), BF16),
            V((n_head - 1, n_exp, rows, width), BF16),
            V((n_exp - 1, rows, width), BF16),
            V((n_exp - 1, rows, width), BF16),
            dma, dma((n_slots,)),
            dma((n_exp,)), dma((n_exp,)), dma((n_exp,)), dma((n_exp,)), dma, dma, dma, dma,
            dma((n_head,)), dma((n_head,)), dma, dma,
            dma((n_exp,)), dma((n_exp,)), dma((n_exp,)), dma((n_exp,)),
            dma((n_head, n_exp)), dma((n_head, n_exp)), dma((n_head,)), dma((n_head,)),
            dma((n_head,)), dma((n_head,)), dma((n_head,)), dma((n_head,)),
            dma((n_head,)), dma((n_head,)), dma((n_head,)), dma((n_head,)),
            dma((n_exp,)), dma((n_exp,)),
        ]
        out = pl.pallas_call(
            functools.partial(kernel, n_tok, n_head, n_exp, n_slots),
            out_shape=jax.ShapeDtypeStruct((rows, width), F32),
            in_specs=[vmem, hbm, vmem, vmem, vmem, vmem, vmem, hbm, hbm, hbm],
            out_specs=vmem,
            scratch_shapes=scratch,
            compiler_params=pltpu.CompilerParams(
                collective_id=0, has_side_effects=True, vmem_limit_bytes=67_043_328
            ),
        )(
            context[0], out_proj, stream[0], norm_gain[None], expert_ids[0].T, slot_ids[0].T,
            gate_probs[0].T, w_gate, w_up, w_down,
        )
        return stream + out[None]

    in_specs = (
        P("exp", "tok", "head"),
        P("head", "exp"),
        P("exp", "tok", "head"),
        P(),
        P("exp", "tok", None),
        P("exp", "tok", None),
        P("exp", "tok", None),
        P(("tok", "exp"), "head", None),
        P(("tok", "exp"), "head", None),
        P(("tok", "exp"), "head", None),
    )
    return jax.shard_map(
        on_device, mesh=mesh, in_specs=in_specs, out_specs=P("exp", "tok", "head"), check_vma=False
    )
```

profile of v0, /device:TPU:0, one launch (start us, length us, event | category | flops | bytes accessed | tf_op | source)
XLA Modules:
  0.0 82.5 jit_solution(6721130567905439664)
XLA Ops:
  0.0 80.8 %shard_map.100 = f32[32,1024]{1,0:T(8,128)} custom-call(bf16[32,1024]{1,0:T(8,128)(2,1)} %bitcast.15, bf16[1024,1024]{1,0:T(8,128)(2,1)} %proj_hbm.1, f32[32,1024]{1,0:T(8,128)} %bitcast.14, f32[1,4096]{1,0:T(1,128)} %bitcast.16, s32[8,32]{1,0:T(8,128)} %bitcast.17, s32[8,32]{1,0:T(8,128)} %bitcast.18, f32[8,32]{1,0:T(8,128)} %bitcast.19, ...), custom_call_target="tpu_custom_call" | custom-call | tf_op jit(solution)/shard_map/pallas_call | solution.py:378
  80.8 1.6 %bitcast_add_fusion = f32[1,32,1024]{2,1,0:T(8,128)} fusion(f32[1,32,1024]{2,1,0:T(8,128)} %param.12, f32[32,1024]{1,0:T(8,128)} %shard_map.100), kind=kLoop, calls=%fused_computation | loop fusion | flops 32768 | bytes 393216 | tf_op jit(solution)/shard_map/add | solution.py:391
where the time goes:
time: 83.5 us; the launch traced here: 82.5 us
  Pallas kernels  80.8 us (97%)
  other arithmetic  1.64 us (2%)
    pallas_call x1, Pallas kernels, on_device(): pl.pallas_call(functools.partial(kernel, n_tok, n_head, n_exp, n_slots),...  80.8 us

commit v1 on v0

v1 whole, which is shorter than its diff:
```python
import functools

import jax
import jax.numpy as jnp
from jax import lax
from jax.experimental import pallas as pl
from jax.experimental.pallas import tpu as pltpu
from jax.sharding import PartitionSpec as P

MESH = pl.DeviceIdType.MESH
LANES = 128
F32 = jnp.float32
BF16 = jnp.bfloat16
eps_value = 1e-05
HALVES = 2


def partner(a, k):
    out, bit = a, 1
    while bit <= k:
        if k & bit:
            out = out + bit - 2 * bit * lax.rem(lax.div(out, bit), 2)
        bit *= 2
    return out


def kernel(
    n_tok, n_head, n_exp,
    ctx_ref, proj_hbm, stream_ref, gain_ref, ids_ref, slots_ref, probs_ref,
    wg_hbm, wu_hbm, wd_hbm,
    out_ref,
    proj, wbuf, ctx_all, wall, stream_bf, stream_t, pbf, pown, prs,
    attn_buf, attn_in, ssq, x, gacc, uacc, hid, acc, own, obf, tin, hsend, hrecv, zsend, zrecv,
    proj_sem, w_sem, l_sem, d_sem, ctx_s, ctx_r, wz_s, wz_r, wt_s, wt_r, st_s, st_r,
    prs_s, prs_r, at_s, at_r, xz_s, xz_r, qz_s, qz_r, xh_s, xh_r, qh_s, qh_r,
    xt_s, xt_r, qt_s, qt_r, to_s, to_r, ho_s, ho_r, zo_s, zo_r,
):
    t, h, e = lax.axis_index("tok"), lax.axis_index("head"), lax.axis_index("exp")
    rows, width = stream_ref.shape
    n_local, n_hid, model = wg_hbm.shape
    depth = ctx_ref.shape[1]
    tokens = n_tok * n_exp * rows
    half = width // HALVES
    turned = {"tok": t, "head": e, "exp": h}
    mine = h == e

    def send(src, dst, s_sem, r_sem, device):
        return pltpu.make_async_remote_copy(
            src_ref=src, dst_ref=dst, send_sem=s_sem, recv_sem=r_sem,
            device_id=device, device_id_type=MESH,
        )

    exp_of = [partner(e, k) for k in range(n_exp)]
    head_of = [partner(h, k) for k in range(n_head)]
    on_exp = [{"exp": i} for i in exp_of]
    on_head = [{"head": i} for i in head_of]
    on_tok = {"tok": 1 - t}

    def lanes(i, size):
        return pl.ds(pl.multiple_of(i * size, min(size, LANES)), size)

    n_part = max(1, n_local - 1)
    n_steps = n_head * HALVES
    proj_c = pltpu.make_async_copy(proj_hbm, proj, proj_sem)
    proj_c.start()

    def w_copy(q):
        source = (wg_hbm, wu_hbm)[q % 2].at[q // 2]
        return pltpu.make_async_copy(source, wbuf.at[q], w_sem.at[q])

    free = [(q, i * width, -1) for q in range(2 * n_part, wbuf.shape[0]) for i in range(n_exp)]
    free += [(q, exp_of[p] * width, p) for p in range(n_exp) for q in range(2 * n_part)]

    def unit(n, size):
        per = width // size
        slot, at, p = free[n // per]
        return slot, pl.ds(pl.multiple_of(at + n % per * size, LANES), size), p

    n_late = (n_local - n_part) * 2 * n_exp

    def late(j, m, i):
        return unit(((j - n_part) * 2 + m) * n_exp + i, width)

    def late_copy(j, m, i):
        slot, cols, _ = late(j, m, i)
        source = (wg_hbm, wu_hbm)[m].at[j, :, pl.ds(i * width, width)]
        return pltpu.make_async_copy(
            source, wbuf.at[slot, :, cols], l_sem.at[((j - n_part) * 2 + m) * n_exp + i]
        )

    steps = [(k, c) for c in range(HALVES) for k in range(n_head - 1, -1, -1)]

    def down(s, j):
        return unit(n_late * HALVES + s * n_local + j, half)

    def d_copy(s, j):
        k, c = steps[s]
        slot, cols, _ = down(s, j)
        return pltpu.make_async_copy(
            wd_hbm.at[j, :, lanes(head_of[k] * HALVES + c, half)],
            wbuf.at[slot, :, cols],
            d_sem.at[s, j],
        )

    def load_after(p):
        for j in range(n_part, n_local):
            for m in range(2):
                for i in range(n_exp):
                    if late(j, m, i)[2] == p:
                        late_copy(j, m, i).start()
        for s in range(n_steps):
            for j in range(n_local):
                if down(s, j)[2] == p:
                    d_copy(s, j).start()

    barrier = pltpu.get_barrier_semaphore()
    for device in on_exp[1:] + on_head[1:] + [on_tok]:
        pl.semaphore_signal(barrier, inc=1, device_id=device, device_id_type=MESH)

    @pl.when(jnp.logical_not(mine))
    def _():
        pl.semaphore_signal(barrier, inc=1, device_id=turned, device_id_type=MESH)

    stream_bf[...] = stream_ref[...].astype(BF16)
    lane = lax.broadcasted_iota(jnp.int32, (rows, LANES), 1)
    n_experts = wall.shape[2]
    expert_row = lax.broadcasted_iota(jnp.int32, (n_experts, rows), 0)
    dense = jnp.zeros((n_experts, rows), F32)
    for k in range(ids_ref.shape[0]):
        hit = (ids_ref[k : k + 1, :] == expert_row) & (slots_ref[k : k + 1, :] >= 0)
        dense = dense + jnp.where(hit, probs_ref[k : k + 1, :], 0.0)
    wall[0, e] = jnp.zeros((n_experts, LANES), F32)
    wall[0, e, :, :rows] = dense

    @pl.when(mine)
    def _():
        pl.semaphore_wait(barrier, n_exp - 1 + n_head - 1 + 1)

    @pl.when(jnp.logical_not(mine))
    def _():
        pl.semaphore_wait(barrier, n_exp - 1 + n_head - 1 + 2)

    order = list(range(n_exp - 1, 0, -1))
    ctx_c = {
        k: send(ctx_ref, ctx_all.at[e], ctx_s.at[k], ctx_r.at[k], on_exp[k]) for k in order
    }
    for k in order:
        ctx_c[k].start()
    stream_c = send(stream_bf, stream_t, st_s, st_r, turned)
    wz_c = [
        send(wall.at[0, e], wall.at[0, e], wz_s.at[k], wz_r.at[k], on_exp[k])
        for k in range(1, n_exp)
    ]
    proj_c.wait()
    for q in range(2 * n_part):
        w_copy(q).start()
    load_after(-1)

    def prs_c(j):
        i = exp_of[j]
        return send(pbf.at[i], prs.at[h], prs_s.at[j], prs_r.at[h], {"head": i})

    tile = min(width, 256)
    for j in [0] + order:
        image = exp_of[j]
        if j:
            ctx_c[j].wait_recv()
        source = ctx_all.at[image] if j else ctx_ref

        def project(i, carry):
            cols = lanes(i, tile)
            part = jnp.dot(source[...], proj[:, cols], preferred_element_type=F32)
            pbf[image, :, cols] = part.astype(BF16)

            @pl.when(image == h)
            def _():
                pown[:, cols] = part

            return carry

        lax.fori_loop(0, width // tile, project, 0)

        @pl.when(image != h)
        def _():
            prs_c(j).start()

        if j == order[0]:

            @pl.when(jnp.logical_not(mine))
            def _():
                stream_c.start()

    for k in range(1, n_head):
        source = head_of[k]
        send(pbf.at[0], prs.at[source], prs_s.at[0], prs_r.at[source], on_head[k]).wait_recv()
    attn = pown[...]
    for k in range(1, n_head):
        attn = attn + prs[head_of[k]].astype(F32)
    attn_buf[...] = attn

    @pl.when(jnp.logical_not(mine))
    def _():
        stream_c.wait()

    @pl.when(mine)
    def _():
        stream_t[...] = stream_bf[...]

    attn_c = send(attn_buf, attn_in, at_s, at_r, turned)

    own_cols = lanes(e, width)
    resid = attn + stream_t[...].astype(F32)
    x[0, h, :, own_cols] = (resid * gain_ref[:, own_cols]).astype(BF16)
    square = jnp.sum(resid * resid, axis=1, keepdims=True)
    row_id = lax.broadcasted_iota(jnp.int32, (rows, LANES), 0)
    flat = jnp.sum(jnp.where(row_id == lane, square, 0.0), axis=0, keepdims=True)
    ssq[0, h, e] = jnp.broadcast_to(flat, (8, LANES))

    def x_at(s, k, j):
        return x.at[s, head_of[k], :, lanes(exp_of[j], width)]

    xz_c = {
        j: send(x_at(0, 0, 0), x_at(0, 0, 0), xz_s.at[j], xz_r.at[j], on_exp[j])
        for j in range(1, n_exp)
    }
    xh_c = {
        (k, j): send(x_at(0, 0, j), x_at(0, 0, j), xh_s.at[k, j], xh_r.at[k, j], on_head[k])
        for k in range(1, n_head) for j in range(n_exp)
    }
    xt_c = {
        (k, j): send(x_at(0, k, j), x_at(1, k, j), xt_s.at[k, j], xt_r.at[k, j], on_tok)
        for k in range(n_head) for j in range(n_exp)
    }
    qz_c = [
        send(ssq.at[0, h, e], ssq.at[0, h, e], qz_s.at[k], qz_r.at[k], on_exp[k])
        for k in range(1, n_exp)
    ]
    qh_c = [
        send(ssq.at[0, h], ssq.at[0, h], qh_s.at[k], qh_r.at[k], on_head[k])
        for k in range(1, n_head)
    ]
    qt_c = send(ssq.at[0], ssq.at[1], qt_s, qt_r, on_tok)
    wt_c = send(wall.at[0], wall.at[1], wt_s, wt_r, on_tok)

    def forward(j):
        if j >= n_exp:
            return
        if j:
            xz_c[j].wait_recv()
        for k in range(1, n_head):
            xh_c[k, j].start()
        xt_c[0, j].start()

    def share(j):
        if j >= n_exp:
            return
        for k in range(1, n_head):
            xh_c[k, j].wait_recv()
            xt_c[k, j].start()

    def small(p):
        if p == 0:
            for c in qz_c:
                c.wait_recv()
            for c in qh_c + wz_c:
                c.start()
        if p == max(1, n_exp - 2):
            for c in qh_c:
                c.wait_recv()
            qt_c.start()
            for c in wz_c:
                c.wait()
            wt_c.start()

            @pl.when(jnp.logical_not(mine))
            def _():
                attn_c.start()

    forward(0)
    for j in range(1, n_exp):
        xz_c[j].start()
    for c in qz_c:
        c.start()
    forward(1)
    share(0)
    forward(2)

    token_row = lax.rem(lax.broadcasted_iota(jnp.int32, (tokens, LANES), 0), rows)
    token_lane = lax.broadcasted_iota(jnp.int32, (tokens, LANES), 1)

    def column(value):
        wide = jnp.broadcast_to(value, (n_tok, n_exp, rows, LANES)).reshape(tokens, LANES)
        return jnp.sum(jnp.where(token_row == token_lane, wide, 0.0), axis=1, keepdims=True)

    hid_tile = 256 if n_hid % 256 == 0 else n_hid
    n_tiles = n_hid // hid_tile
    dims = (((1,), (1,)), ((), ()))

    def factors(j):
        sums = column(jnp.sum(ssq[...], axis=2)[:, :, 0:1, :])
        scale = lax.rsqrt(sums / model + eps_value)
        number = (t * n_exp + e) * n_local + j
        expert_of = lax.broadcasted_iota(jnp.int32, wall.shape, 2)
        picked = jnp.where(expert_of == number, wall[...], 0.0)
        return scale, column(jnp.sum(picked, axis=2, keepdims=True))

    def finish(q, g, u, scale, gate_w):
        g = g * scale
        u = u * scale
        hid[q] = (g / (1.0 + jnp.exp(-g)) * u * gate_w).astype(BF16)

    def up_part(j, p):
        cols = lanes(exp_of[p], width)
        scale, gate_w = factors(j) if p == n_exp - 1 else (None, None)

        def body(i, carry):
            q = j * n_tiles + i
            span = lanes(i, hid_tile)
            xv = x[:, :, :, cols].reshape(tokens, width)
            g = lax.dot_general(xv, wbuf[2 * j, span, cols], dims, preferred_element_type=F32)
            u = lax.dot_general(xv, wbuf[2 * j + 1, span, cols], dims, preferred_element_type=F32)
            if p:
                g = g + gacc[q]
                u = u + uacc[q]
            if p < n_exp - 1:
                gacc[q] = g
                uacc[q] = u
            else:
                finish(q, g, u, scale, gate_w)
            return carry

        lax.fori_loop(0, n_tiles, body, 0, unroll=True)

    def up_whole(j):
        scale, gate_w = factors(j)

        def body(i, carry):
            span = lanes(i, hid_tile)
            both = []
            for m in range(2):
                value = jnp.zeros((tokens, hid_tile), F32)
                for n in range(n_exp):
                    slot, cols, _ = late(j, m, n)
                    value = value + lax.dot_general(
                        x[:, :, :, n * width : (n + 1) * width].reshape(tokens, width),
                        wbuf[slot, span, cols], dims, preferred_element_type=F32,
                    )
                both.append(value)
            finish(j * n_tiles + i, both[0], both[1], scale, gate_w)
            return carry

        lax.fori_loop(0, n_tiles, body, 0, unroll=True)

    for p in range(n_exp):
        for k in range(n_head):
            xt_c[k, p].wait_recv()
        if p == n_exp - 1:
            qt_c.wait_recv()
            wt_c.wait()
        for j in range(n_part):
            if p == 0:
                w_copy(2 * j).wait()
                w_copy(2 * j + 1).wait()
            up_part(j, p)
            if j == 0:
                forward(p + 3)
                small(p)
            if j == max(0, n_part - 2):
                share(p + 1)
        load_after(p)
    for j in range(n_part, n_local):
        for m in range(2):
            for i in range(n_exp):
                late_copy(j, m, i).wait()
        up_whole(j)

    to_c = [send(obf.at[s], tin.at[s], to_s.at[s], to_r.at[s], on_tok) for s in range(n_steps)]
    group = n_exp // 2
    near = lax.div(e, group) * group
    first_of = (near, (n_exp - group) - near)

    def ho_c(k, c, g):
        at = (c, k - 1, pl.ds(first_of[g], group))
        return send(hsend.at[at], hrecv.at[at], ho_s.at[k, c, g], ho_r.at[k, c, g], on_head[k])

    def zo_c(m, c):
        at = (c, m - 1)
        return send(zsend.at[at], zrecv.at[at], zo_s.at[m, c], zo_r.at[m, c], on_exp[m])

    def head_step(s):
        k, c = steps[s]
        to_c[s].wait_recv()
        if k:
            hsend[c, k - 1] = (acc[s % 2] + tin[s].astype(F32)).astype(BF16)
            for g in (1, 0):
                ho_c(k, c, g).start()
        else:
            own[c] = acc[s % 2] + tin[s].astype(F32)

    def summed(m, c):
        value = own[c, exp_of[m]]
        for k in range(1, n_head):
            value = value + hrecv[c, k - 1, exp_of[m]].astype(F32)
        return value

    def exp_step(c):
        for m in range(n_exp - 1, 0, -1):
            if m in (n_exp - 1, group - 1):
                for k in range(1, n_head):
                    ho_c(k, c, m // group).wait_recv()
            zsend[c, m - 1] = summed(m, c).astype(BF16)
            zo_c(m, c).start()

    for s in range(n_steps):
        for j in range(n_local):
            d_copy(s, j).wait()
        value = jnp.zeros((tokens, half), F32)
        for j in range(n_local):
            slot, cols, _ = down(s, j)
            for i in range(n_tiles):
                value = value + jnp.dot(
                    hid[j * n_tiles + i],
                    wbuf[slot, i * hid_tile : (i + 1) * hid_tile, cols],
                    preferred_element_type=F32,
                )
        value = value.reshape(n_tok, n_exp, rows, half)
        acc[s % 2] = value[0]
        obf[s] = value[1].astype(BF16)
        to_c[s].start()
        if s:
            head_step(s - 1)
    head_step(n_steps - 1)
    for c in list(ctx_c.values()) + list(xz_c.values()) + qz_c + list(xh_c.values()) + qh_c:
        c.wait_send()
    for c in list(xt_c.values()) + [qt_c] + to_c:
        c.wait_send()
    for j in range(n_exp):

        @pl.when(exp_of[j] != h)
        def _():
            prs_c(j).wait_send()

    for c in range(HALVES):
        exp_step(c)

    @pl.when(jnp.logical_not(mine))
    def _():
        attn_c.wait()

    @pl.when(mine)
    def _():
        attn_in[...] = attn_buf[...]

    for c in range(HALVES):
        if group == 1:
            for k in range(1, n_head):
                ho_c(k, c, 0).wait_recv()
        value = summed(0, c) + attn_in[:, c * half : (c + 1) * half]
        for m in range(n_exp - 1, 0, -1):
            zo_c(m, c).wait_recv()
            value = value + zrecv[c, m - 1].astype(F32)
        out_ref[:, c * half : (c + 1) * half] = value

    for c in range(HALVES):
        for k in range(1, n_head):
            for g in range(2):
                ho_c(k, c, g).wait_send()
        for m in range(1, n_exp):
            zo_c(m, c).wait_send()


def solution(mesh):
    n_tok, n_head, n_exp = mesh.shape["tok"], mesh.shape["head"], mesh.shape["exp"]

    def on_device(
        context, out_proj, stream, norm_gain, expert_ids, slot_ids, gate_probs, w_gate, w_up, w_down
    ):
        rows, width = stream.shape[1:]
        n_local, n_hid, model = w_gate.shape
        tokens = n_tok * n_exp * rows
        depth = context.shape[2]
        half = width // HALVES
        n_steps = n_head * HALVES
        hid_tile = 256 if n_hid % 256 == 0 else n_hid
        n_tiles = n_hid // hid_tile
        n_part = max(1, n_local - 1)
        vmem = pl.BlockSpec(memory_space=pltpu.VMEM)
        hbm = pl.BlockSpec(memory_space=pl.ANY)
        dma = pltpu.SemaphoreType.DMA
        V = pltpu.VMEM
        n_slots = max(2 * n_part, 3 * n_local - 2 * n_part)
        n_late = (n_local - n_part) * 2 * n_exp
        scratch = [
            V(out_proj.shape, BF16),
            V((n_slots, n_hid, model), BF16),
            V((n_exp, rows, depth), BF16),
            V((n_tok, n_exp, n_tok * n_exp * n_local, LANES), F32),
            V((rows, width), BF16),
            V((rows, width), BF16),
            V((n_exp, rows, width), BF16),
            V((rows, width), F32),
            V((n_head, rows, width), BF16),
            V((rows, width), F32),
            V((rows, width), F32),
            V((n_tok, n_exp, n_exp, 8, LANES), F32),
            V((n_tok, n_exp, rows, model), BF16),
            V((n_part * n_tiles, tokens, hid_tile), F32),
            V((n_part * n_tiles, tokens, hid_tile), F32),
            V((n_local * n_tiles, tokens, hid_tile), BF16),
            V((2, n_exp, rows, half), F32),
            V((HALVES, n_exp, rows, half), F32),
            V((n_steps, n_exp, rows, half), BF16),
            V((n_steps, n_exp, rows, half), BF16),
            V((HALVES, n_head - 1, n_exp, rows, half), BF16),
            V((HALVES, n_head - 1, n_exp, rows, half), BF16),
            V((HALVES, n_exp - 1, rows, half), BF16),
            V((HALVES, n_exp - 1, rows, half), BF16),
            dma, dma((2 * n_part,)), dma((max(1, n_late),)), dma((n_steps, n_local)),
            dma((n_exp,)), dma((n_exp,)), dma((n_exp,)), dma((n_exp,)), dma, dma, dma, dma,
            dma((n_exp,)), dma((n_head,)), dma, dma,
            dma((n_exp,)), dma((n_exp,)), dma((n_exp,)), dma((n_exp,)),
            dma((n_head, n_exp)), dma((n_head, n_exp)), dma((n_head,)), dma((n_head,)),
            dma((n_head, n_exp)), dma((n_head, n_exp)), dma, dma,
            dma((n_steps,)), dma((n_steps,)),
            dma((n_head, HALVES, 2)), dma((n_head, HALVES, 2)),
            dma((n_exp, HALVES)), dma((n_exp, HALVES)),
        ]
        out = pl.pallas_call(
            functools.partial(kernel, n_tok, n_head, n_exp),
            out_shape=jax.ShapeDtypeStruct((rows, width), F32),
            in_specs=[vmem, hbm, vmem, vmem, vmem, vmem, vmem, hbm, hbm, hbm],
            out_specs=vmem,
            scratch_shapes=scratch,
            compiler_params=pltpu.CompilerParams(
                collective_id=0, has_side_effects=True, vmem_limit_bytes=67_043_328
            ),
        )(
            context[0], out_proj, stream[0], norm_gain[None], expert_ids[0].T, slot_ids[0].T,
            gate_probs[0].T, w_gate, w_up, w_down,
        )
        return stream + out[None]

    in_specs = (
        P("exp", "tok", "head"),
        P("head", "exp"),
        P("exp", "tok", "head"),
        P(),
        P("exp", "tok", None),
        P("exp", "tok", None),
        P("exp", "tok", None),
        P(("tok", "exp"), "head", None),
        P(("tok", "exp"), "head", None),
        P(("tok", "exp"), "head", None),
    )
    return jax.shard_map(
        on_device, mesh=mesh, in_specs=in_specs, out_specs=P("exp", "tok", "head"), check_vma=False
    )
```

time: 83.5 us -> 67.6 us (0.81); the launches traced: 82.5 us -> 67.5 us
  Pallas kernels: 80.8 us -> 65.8 us
    pallas_call x1, Pallas kernels: 80.8 us -> 65.8 us  [on_device(): pl.pallas_call(functools.partial(kernel, n_tok, n_head, n_exp), out_shape...]
where the time goes in v1:
time: 67.6 us; the launch traced here: 67.5 us
  Pallas kernels  65.8 us (97%)
  other arithmetic  1.64 us (2%)
    pallas_call x1, Pallas kernels, on_device(): pl.pallas_call(functools.partial(kernel, n_tok, n_head, n_exp), out_shape...  65.8 us
    add x1, other arithmetic, on_device(): return stream + out[None]  1.64 us

profile of v1, /device:TPU:0, one launch (start us, length us, event | category | flops | bytes accessed | tf_op | source)
XLA Modules:
  0.0 67.5 jit_solution(5051103116244787246)
XLA Ops:
  0.0 65.8 %shard_map.100 = f32[32,1024]{1,0:T(8,128)} custom-call(bf16[32,1024]{1,0:T(8,128)(2,1)} %bitcast.15, bf16[1024,1024]{1,0:T(8,128)(2,1)} %proj_hbm.1, f32[32,1024]{1,0:T(8,128)} %bitcast.14, f32[1,4096]{1,0:T(1,128)} %bitcast.16, s32[8,32]{1,0:T(8,128)} %bitcast.17, s32[8,32]{1,0:T(8,128)} %bitcast.18, f32[8,32]{1,0:T(8,128)} %bitcast.19, ...), custom_call_target="tpu_custom_call" | custom-call | tf_op jit(solution)/shard_map/pallas_call | solution.py:528
  65.8 1.6 %bitcast_add_fusion = f32[1,32,1024]{2,1,0:T(8,128)} fusion(f32[1,32,1024]{2,1,0:T(8,128)} %param.12, f32[32,1024]{1,0:T(8,128)} %shard_map.100), kind=kLoop, calls=%fused_computation | loop fusion | flops 32768 | bytes 393216 | tf_op jit(solution)/shard_map/add | solution.py:541

commit v2 on v1

v2 whole, which is shorter than its diff:
```python
import functools

import jax
import jax.numpy as jnp
from jax import lax
from jax.experimental import pallas as pl
from jax.experimental.pallas import tpu as pltpu
from jax.sharding import PartitionSpec as P

MESH = pl.DeviceIdType.MESH
LANES = 128
F32 = jnp.float32
BF16 = jnp.bfloat16
eps_value = 1e-05
VMEM_BYTES = 62_500_000


def parts_of(width):
    sizes = (width // 2, width // 4, width // 4) if width % 512 == 0 else (width // 2, width // 2)
    return [(sum(sizes[:i]), size) for i, size in enumerate(sizes)]


def steps_of(width, n_head):
    far, middle = n_head - 1, n_head // 2
    first = [k for k in range(far - 1, 0, -1)] + [far, 0]
    rest = [middle] + [k for k in range(far, 0, -1) if k != middle] + [0]
    return [(k, c) for c in range(len(parts_of(width))) for k in (rest if c else first)]


def partner(a, k):
    out, bit = a, 1
    while bit <= k:
        if k & bit:
            out = out + bit - 2 * bit * lax.rem(lax.div(out, bit), 2)
        bit *= 2
    return out


def kernel(
    n_tok, n_head, n_exp,
    ctx_ref, proj_hbm, stream_ref, gain_ref, ids_ref, slots_ref, probs_ref,
    wg_hbm, wu_hbm, wd_hbm,
    out_ref,
    proj, wbuf, ctx_all, wall, stream_bf, stream_t, pbf, pown, prs,
    attn_buf, attn_in, ssq, x, gacc, uacc, hid, acc, own, obf, tin, hsend, hrecv, zsend, zrecv,
    fown, fzsend, fzrecv, fsend, frecv,
    proj_sem, w_sem, l_sem, d_sem, ctx_s, ctx_r, wz_s, wz_r, wt_s, wt_r, st_s, st_r,
    prs_s, prs_r, at_s, at_r, xz_s, xz_r, qz_s, qz_r, xh_s, xh_r, qh_s, qh_r,
    xt_s, xt_r, qt_s, qt_r, to_s, to_r, ho_s, ho_r, zo_s, zo_r, fz_s, fz_r, fh_s, fh_r,
):
    t, h, e = lax.axis_index("tok"), lax.axis_index("head"), lax.axis_index("exp")
    rows, width = stream_ref.shape
    n_local, n_hid, model = wg_hbm.shape
    depth = ctx_ref.shape[1]
    tokens = n_tok * n_exp * rows
    parts = parts_of(width)
    turned = {"tok": t, "head": e, "exp": h}
    mine = h == e

    def send(src, dst, s_sem, r_sem, device):
        return pltpu.make_async_remote_copy(
            src_ref=src, dst_ref=dst, send_sem=s_sem, recv_sem=r_sem,
            device_id=device, device_id_type=MESH,
        )

    def sent(ref, sem):
        send(ref, ref, sem, sem, {"tok": 1 - t}).wait_send()

    def arrived(ref, sem):
        send(ref, ref, sem, sem, {"tok": 1 - t}).wait_recv()

    def loaded(ref, sem):
        pltpu.make_async_copy(ref, ref, sem).wait()

    exp_of = [partner(e, k) for k in range(n_exp)]
    head_of = [partner(h, k) for k in range(n_head)]
    on_exp = [{"exp": i} for i in exp_of]
    on_head = [{"head": i} for i in head_of]
    on_tok = {"tok": 1 - t}

    def lanes(i, size):
        return pl.ds(pl.multiple_of(i * size, min(size, LANES)), size)

    n_part = max(1, n_local - 1)
    steps = steps_of(width, n_head)
    n_steps = len(steps)
    proj_c = pltpu.make_async_copy(proj_hbm, proj, proj_sem)
    proj_c.start()

    def w_copy(q):
        source = (wg_hbm, wu_hbm)[q % 2].at[q // 2]
        return pltpu.make_async_copy(source, wbuf.at[q], w_sem.at[q // 2])

    free = [(q, i * width, -1) for q in range(2 * n_part, wbuf.shape[0]) for i in range(n_exp)]
    free += [(q, exp_of[p] * width, p) for p in range(n_exp) for q in range(2 * n_part)]

    def place(at, size):
        slot, first, p = free[at // width]
        return slot, pl.ds(pl.multiple_of(first + at % width, LANES), size), p

    n_late = (n_local - n_part) * 2 * n_exp

    def late(j, m, i):
        return place((((j - n_part) * 2 + m) * n_exp + i) * width, width)

    def late_copy(j, m, i):
        slot, cols, _ = late(j, m, i)
        source = (wg_hbm, wu_hbm)[m].at[j, :, pl.ds(i * width, width)]
        return pltpu.make_async_copy(
            source, wbuf.at[slot, :, cols], l_sem.at[j - n_part]
        )

    down_at, at = {}, n_late * width
    for n, (_, c) in enumerate(steps):
        for j in range(n_local):
            down_at[n, j] = at
            at += parts[c][1]

    def down(s, j):
        return place(down_at[s, j], parts[steps[s][1]][1])

    def d_copy(s, j):
        k, c = steps[s]
        slot, cols, _ = down(s, j)
        first, size = parts[c]
        source = wd_hbm.at[j, :, pl.ds(pl.multiple_of(head_of[k] * width + first, LANES), size)]
        return pltpu.make_async_copy(source, wbuf.at[slot, :, cols], d_sem.at[s])

    def load_after(p):
        for j in range(n_part, n_local):
            for m in range(2):
                for i in range(n_exp):
                    if late(j, m, i)[2] == p:
                        late_copy(j, m, i).start()
        for s in range(n_steps):
            for j in range(n_local):
                if down(s, j)[2] == p:
                    d_copy(s, j).start()

    barrier = pltpu.get_barrier_semaphore()
    for device in on_exp[1:] + on_head[1:] + [on_tok]:
        pl.semaphore_signal(barrier, inc=1, device_id=device, device_id_type=MESH)

    @pl.when(jnp.logical_not(mine))
    def _():
        pl.semaphore_signal(barrier, inc=1, device_id=turned, device_id_type=MESH)

    stream_bf[...] = stream_ref[...].astype(BF16)
    lane = lax.broadcasted_iota(jnp.int32, (rows, LANES), 1)
    n_experts = wall.shape[2]
    expert_row = lax.broadcasted_iota(jnp.int32, (n_experts, rows), 0)
    dense = jnp.zeros((n_experts, rows), F32)
    for k in range(ids_ref.shape[0]):
        hit = (ids_ref[k : k + 1, :] == expert_row) & (slots_ref[k : k + 1, :] >= 0)
        dense = dense + jnp.where(hit, probs_ref[k : k + 1, :], 0.0)
    wall[0, e] = jnp.zeros((n_experts, LANES), F32)
    wall[0, e, :, :rows] = dense

    @pl.when(mine)
    def _():
        pl.semaphore_wait(barrier, n_exp - 1 + n_head - 1 + 1)

    @pl.when(jnp.logical_not(mine))
    def _():
        pl.semaphore_wait(barrier, n_exp - 1 + n_head - 1 + 2)

    order = list(range(n_exp - 1, 0, -1))
    ctx_c = {
        k: send(ctx_ref, ctx_all.at[e], ctx_s, ctx_r.at[k], on_exp[k]) for k in order
    }
    for k in order:
        ctx_c[k].start()
    stream_c = send(stream_bf, stream_t, st_s, st_r, turned)
    wz_c = [
        send(wall.at[0, e], wall.at[0, e], wz_s, wz_r, on_exp[k])
        for k in range(1, n_exp)
    ]
    proj_c.wait()
    for q in range(2 * n_part):
        w_copy(q).start()
    load_after(-1)

    def prs_c(j):
        i = exp_of[j]
        return send(pbf.at[i], prs.at[h], prs_s, prs_r, {"head": i})

    tile = min(width, 256)
    for group in [[0]] + [order[:1]] + [order[i : i + 2] for i in range(1, len(order), 2)]:
        pieces = []
        for j in group:
            if j:
                ctx_c[j].wait_recv()
            pieces.append(ctx_all[exp_of[j]] if j else ctx_ref[...])
        pieces = jnp.concatenate(pieces, axis=0)

        def project(i, carry):
            cols = lanes(i, tile)
            part = jnp.dot(pieces, proj[:, cols], preferred_element_type=F32)
            for n, j in enumerate(group):
                mine_part = part[n * rows : (n + 1) * rows]
                pbf[exp_of[j], :, cols] = mine_part.astype(BF16)

                @pl.when(exp_of[j] == h)
                def _():
                    pown[:, cols] = mine_part

            return carry

        lax.fori_loop(0, width // tile, project, 0, unroll=True)
        for j in group:

            @pl.when(exp_of[j] != h)
            def _():
                prs_c(j).start()

        if group == order[:1]:

            @pl.when(jnp.logical_not(mine))
            def _():
                stream_c.start()

    arrived(prs.at[pl.ds(0, n_head - 1)], prs_r)
    attn = pown[...]
    for k in range(1, n_head):
        attn = attn + prs[head_of[k]].astype(F32)
    attn_buf[...] = attn

    @pl.when(jnp.logical_not(mine))
    def _():
        stream_c.wait()

    @pl.when(mine)
    def _():
        stream_t[...] = stream_bf[...]

    attn_c = send(attn_buf, attn_in, at_s, at_r, turned)

    own_cols = lanes(e, width)
    resid = attn + stream_t[...].astype(F32)
    x[0, h, :, own_cols] = (resid * gain_ref[:, own_cols]).astype(BF16)
    square = jnp.sum(resid * resid, axis=1, keepdims=True)
    row_id = lax.broadcasted_iota(jnp.int32, (rows, LANES), 0)
    flat = jnp.sum(jnp.where(row_id == lane, square, 0.0), axis=0, keepdims=True)
    ssq[0, h, e] = jnp.broadcast_to(flat, (8, LANES))

    def x_at(s, k, j):
        return x.at[s, head_of[k], :, lanes(exp_of[j], width)]

    xz_c = {
        j: send(x_at(0, 0, 0), x_at(0, 0, 0), xz_s, xz_r.at[j], on_exp[j])
        for j in range(1, n_exp)
    }
    xh_c = {
        (k, j): send(x_at(0, 0, j), x_at(0, 0, j), xh_s, xh_r.at[k - 1, j], on_head[k])
        for k in range(1, n_head) for j in range(n_exp)
    }
    xt_c = {
        (k, j): send(x_at(0, k, j), x_at(1, k, j), xt_s, xt_r.at[j], on_tok)
        for k in range(n_head) for j in range(n_exp)
    }
    qz_c = [
        send(ssq.at[0, h, e], ssq.at[0, h, e], qz_s, qz_r, on_exp[k])
        for k in range(1, n_exp)
    ]
    qh_c = [
        send(ssq.at[0, h], ssq.at[0, h], qh_s, qh_r, on_head[k])
        for k in range(1, n_head)
    ]
    qt_c = send(ssq.at[0], ssq.at[1], qt_s, qt_r, on_tok)
    wt_c = send(wall.at[0], wall.at[1], wt_s, wt_r, on_tok)

    def forward(j):
        if j >= n_exp:
            return
        if j:
            xz_c[j].wait_recv()
        for k in range(1, n_head):
            xh_c[k, j].start()
        xt_c[0, j].start()

    def share(j):
        if j >= n_exp:
            return
        for k in range(1, n_head):
            xh_c[k, j].wait_recv()
            xt_c[k, j].start()

    def small(p):
        if p == 0:
            arrived(ssq.at[0, 0, pl.ds(0, n_exp - 1)], qz_r)
            for c in qh_c + wz_c:
                c.start()
        if p == max(1, n_exp - 2):
            arrived(ssq.at[0, pl.ds(0, n_head - 1)], qh_r)
            qt_c.start()
            arrived(wall.at[0, pl.ds(0, n_exp - 1)], wz_r)
            wt_c.start()

            @pl.when(jnp.logical_not(mine))
            def _():
                attn_c.start()

    forward(0)
    for j in range(1, n_exp):
        xz_c[j].start()
    for c in qz_c:
        c.start()
    forward(1)
    share(0)
    forward(2)

    token_row = lax.rem(lax.broadcasted_iota(jnp.int32, (tokens, LANES), 0), rows)
    token_lane = lax.broadcasted_iota(jnp.int32, (tokens, LANES), 1)

    def column(value):
        wide = jnp.broadcast_to(value, (n_tok, n_exp, rows, LANES)).reshape(tokens, LANES)
        return jnp.sum(jnp.where(token_row == token_lane, wide, 0.0), axis=1, keepdims=True)

    hid_tile = 256 if n_hid % 256 == 0 else n_hid
    n_tiles = n_hid // hid_tile
    dims = (((1,), (1,)), ((), ()))

    def factors(j):
        sums = column(jnp.sum(ssq[...], axis=2)[:, :, 0:1, :])
        scale = lax.rsqrt(sums / model + eps_value)
        number = (t * n_exp + e) * n_local + j
        expert_of = lax.broadcasted_iota(jnp.int32, wall.shape, 2)
        picked = jnp.where(expert_of == number, wall[...], 0.0)
        return scale, column(jnp.sum(picked, axis=2, keepdims=True))

    def finish(j, i, g, u, scale, gate_w):
        g = g * scale
        u = u * scale
        hid[j, :, lanes(i, hid_tile)] = (g / (1.0 + jnp.exp(-g)) * u * gate_w).astype(BF16)

    def up_part(j, p):
        cols = lanes(exp_of[p], width)
        scale, gate_w = factors(j) if p == n_exp - 1 else (None, None)

        def body(i, carry):
            q = j * n_tiles + i
            span = lanes(i, hid_tile)
            xv = x[:, :, :, cols].reshape(tokens, width)
            g = lax.dot_general(xv, wbuf[2 * j, span, cols], dims, preferred_element_type=F32)
            u = lax.dot_general(xv, wbuf[2 * j + 1, span, cols], dims, preferred_element_type=F32)
            if p:
                g = g + gacc[q]
                u = u + uacc[q]
            if p < n_exp - 1:
                gacc[q] = g
                uacc[q] = u
            else:
                finish(j, i, g, u, scale, gate_w)
            return carry

        lax.fori_loop(0, n_tiles, body, 0, unroll=True)

    def up_whole(j):
        scale, gate_w = factors(j)

        def body(i, carry):
            span = lanes(i, hid_tile)
            both = []
            for m in range(2):
                value = jnp.zeros((tokens, hid_tile), F32)
                for n in range(n_exp):
                    slot, cols, _ = late(j, m, n)
                    value = value + lax.dot_general(
                        x[:, :, :, n * width : (n + 1) * width].reshape(tokens, width),
                        wbuf[slot, span, cols], dims, preferred_element_type=F32,
                    )
                both.append(value)
            finish(j, i, both[0], both[1], scale, gate_w)
            return carry

        lax.fori_loop(0, n_tiles, body, 0, unroll=True)

    for p in range(n_exp):
        arrived(pbf, xt_r.at[p])
        if p == n_exp - 1:
            qt_c.wait_recv()
            wt_c.wait_recv()
        for j in range(n_part):
            if p == 0:
                loaded(wbuf.at[pl.ds(0, 2)], w_sem.at[j])
            up_part(j, p)
            if j == 0:
                forward(p + 3)
                small(p)
            if j == max(0, n_part - 2):
                share(p + 1)
        load_after(p)
    for j in range(n_part, n_local):
        loaded(wbuf.at[pl.ds(0, 2)], l_sem.at[j - n_part])
        up_whole(j)

    far = n_head - 1
    to_c = [
        send(obf[c].at[k], tin[c].at[k], to_s.at[c], to_r.at[k, c], on_tok) for k, c in steps
    ]
    group = n_exp // 2
    near = lax.div(e, group) * group
    first_of = (near, (n_exp - group) - near)

    def heads_of(c):
        return range(1, n_head) if c else range(1, far)

    def ho_c(k, c, g):
        at = (k - 1, pl.ds(first_of[g], group))
        return send(
            hsend[c].at[at], hrecv[c].at[at], ho_s.at[c], ho_r.at[c, g], on_head[k]
        )

    def zo_c(m, c):
        return send(zsend[c].at[m - 1], zrecv[c].at[m - 1], zo_s.at[c], zo_r.at[c], on_exp[m])

    def heads_arrived(c, g):
        arrived(hrecv[c].at[pl.ds(0, len(heads_of(c))), pl.ds(0, group)], ho_r.at[c, g])

    fz_c = [
        send(fzsend.at[m - 1], fzrecv.at[m - 1], fz_s, fz_r, on_exp[m])
        for m in range(1, n_exp)
    ]
    fh_c = send(fsend, frecv, fh_s, fh_r, on_head[far])

    def head_step(s):
        k, c = steps[s]
        to_c[s].wait_recv()
        if k == far and c == 0:
            for m in range(n_exp - 1, -1, -1):
                i = exp_of[m]
                value = acc[c][s % 4, i] + tin[c][k, i].astype(F32)
                if m:
                    fzsend[m - 1] = value.astype(BF16)
                    fz_c[m - 1].start()
                else:
                    fown[...] = value
        elif k:
            hsend[c][k - 1] = (acc[c][s % 4] + tin[c][k].astype(F32)).astype(BF16)
            for g in (1, 0):
                ho_c(k, c, g).start()
        else:
            own[c][...] = acc[c][s % 4] + tin[c][k].astype(F32)

    def far_step():
        value = fown[...]
        arrived(fzrecv, fz_r)
        for m in range(n_exp - 1, 0, -1):
            value = value + fzrecv[m - 1].astype(F32)
        fsend[...] = value.astype(BF16)
        fh_c.start()

    def summed(m, c):
        value = own[c][exp_of[m]]
        for k in heads_of(c):
            value = value + hrecv[c][k - 1, exp_of[m]].astype(F32)
        return value

    def exp_step(c):
        for m in range(n_exp - 1, 0, -1):
            if m in (n_exp - 1, group - 1):
                heads_arrived(c, m // group)
            zsend[c][m - 1] = summed(m, c).astype(BF16)
            zo_c(m, c).start()

    def down_steps(batch):
        size = parts[steps[batch[0]][1]][1]
        for s in batch:
            loaded(wbuf.at[0, :, pl.ds(0, n_local * size)], d_sem.at[s])
        values = [jnp.zeros((tokens, size), F32) for _ in batch]
        for j in range(n_local):
            for n, s in enumerate(batch):
                slot, cols, _ = down(s, j)
                values[n] = values[n] + jnp.dot(
                    hid[j], wbuf[slot, :, cols], preferred_element_type=F32
                )
        for s, value in zip(batch, values):
            k, c = steps[s]
            value = value.reshape(n_tok, n_exp, rows, size)
            acc[c][s % 4] = value[0]
            obf[c][k] = value[1].astype(BF16)
            to_c[s].start()

    batches, s = [], 0
    while s < n_steps:
        n = 1 if parts[steps[s][1]][1] > 256 else 2
        batches.append(range(s, s + n))
        s += n
    for b, batch in enumerate(batches):
        down_steps(batch)
        for s in batches[b - 1] if b else ():
            head_step(s)
        if len(parts) > 2 and batch[-1] == 2 * n_head + 1:
            exp_step(0)
    for s in batches[-1]:
        head_step(s)
    some = pl.ds(0, n_exp - 1)
    sent(ctx_all.at[some], ctx_s)
    sent(pbf.at[some], prs_s)
    sent(pbf.at[some], xz_s)
    sent(x.at[0, pl.ds(0, n_head - 1)], xh_s)
    sent(x.at[0], xt_s)
    sent(ssq.at[0, 0, some], qz_s)
    sent(ssq.at[0, pl.ds(0, n_head - 1)], qh_s)
    sent(wall.at[0, some], wz_s)
    wt_c.wait_send()
    qt_c.wait_send()
    far_step()
    for c in range(1 if len(parts) > 2 else 0, len(parts)):
        exp_step(c)

    @pl.when(jnp.logical_not(mine))
    def _():
        attn_c.wait()

    @pl.when(mine)
    def _():
        attn_in[...] = attn_buf[...]

    for c, (first, size) in enumerate(parts):
        if group == 1:
            heads_arrived(c, 0)
        value = summed(0, c) + attn_in[:, first : first + size]
        if c == 0:
            fh_c.wait_recv()
            value = value + frecv[...].astype(F32)
        arrived(zrecv[c], zo_r.at[c])
        for m in range(n_exp - 1, 0, -1):
            value = value + zrecv[c][m - 1].astype(F32)
        out_ref[:, first : first + size] = value

    for c in range(len(parts)):
        sent(obf[c], to_s.at[c])
        sent(hsend[c].at[pl.ds(0, len(heads_of(c)))], ho_s.at[c])
        sent(zsend[c], zo_s.at[c])
    sent(fzsend, fz_s)
    fh_c.wait_send()


def solution(mesh):
    n_tok, n_head, n_exp = mesh.shape["tok"], mesh.shape["head"], mesh.shape["exp"]

    def on_device(
        context, out_proj, stream, norm_gain, expert_ids, slot_ids, gate_probs, w_gate, w_up, w_down
    ):
        rows, width = stream.shape[1:]
        n_local, n_hid, model = w_gate.shape
        tokens = n_tok * n_exp * rows
        depth = context.shape[2]
        parts = parts_of(width)
        n_parts = len(parts)
        n_steps = len(steps_of(width, n_head))
        hid_tile = 256 if n_hid % 256 == 0 else n_hid
        n_tiles = n_hid // hid_tile
        n_part = max(1, n_local - 1)
        vmem = pl.BlockSpec(memory_space=pltpu.VMEM)
        hbm = pl.BlockSpec(memory_space=pl.ANY)
        dma = pltpu.SemaphoreType.DMA
        V = pltpu.VMEM
        n_slots = max(2 * n_part, 3 * n_local - 2 * n_part)
        scratch = [
            V(out_proj.shape, BF16),
            V((n_slots, n_hid, model), BF16),
            V((n_exp, rows, depth), BF16),
            V((n_tok, n_exp, n_tok * n_exp * n_local, LANES), F32),
            V((rows, width), BF16),
            V((rows, width), BF16),
            V((n_exp, rows, width), BF16),
            V((rows, width), F32),
            V((n_head, rows, width), BF16),
            V((rows, width), F32),
            V((rows, width), F32),
            V((n_tok, n_exp, n_exp, 8, LANES), F32),
            V((n_tok, n_exp, rows, model), BF16),
            V((n_part * n_tiles, tokens, hid_tile), F32),
            V((n_part * n_tiles, tokens, hid_tile), F32),
            V((n_local, tokens, n_hid), BF16),
            [V((4, n_exp, rows, size), F32) for _, size in parts],
            [V((n_exp, rows, size), F32) for _, size in parts],
            [V((n_head, n_exp, rows, size), BF16) for _, size in parts],
            [V((n_head, n_exp, rows, size), BF16) for _, size in parts],
            [V((n_head - 1, n_exp, rows, size), BF16) for _, size in parts],
            [V((n_head - 1, n_exp, rows, size), BF16) for _, size in parts],
            [V((n_exp - 1, rows, size), BF16) for _, size in parts],
            [V((n_exp - 1, rows, size), BF16) for _, size in parts],
            V((rows, parts[0][1]), F32),
            V((n_exp - 1, rows, parts[0][1]), BF16),
            V((n_exp - 1, rows, parts[0][1]), BF16),
            V((rows, parts[0][1]), BF16),
            V((rows, parts[0][1]), BF16),
            dma, dma((n_part,)), dma((max(1, n_local - n_part),)), dma((n_steps,)),
            dma, dma((n_exp,)), dma, dma, dma, dma, dma, dma,
            dma, dma, dma, dma,
            dma, dma((n_exp,)), dma, dma, dma, dma((n_head - 1, n_exp)), dma, dma,
            dma, dma((n_exp,)), dma, dma,
            dma((n_parts,)), dma((n_head, n_parts)), dma((n_parts,)), dma((n_parts, 2)),
            dma((n_parts,)), dma((n_parts,)), dma, dma, dma, dma,
        ]
        out = pl.pallas_call(
            functools.partial(kernel, n_tok, n_head, n_exp),
            out_shape=pltpu.VMEM((rows, width), F32),
            in_specs=[vmem, hbm, vmem, vmem, vmem, vmem, vmem, hbm, hbm, hbm],
            out_specs=vmem,
            scratch_shapes=scratch,
            compiler_params=pltpu.CompilerParams(
                collective_id=0, has_side_effects=True, vmem_limit_bytes=VMEM_BYTES
            ),
        )(
            context[0], out_proj, stream[0], norm_gain[None], expert_ids[0].T, slot_ids[0].T,
            gate_probs[0].T, w_gate, w_up, w_down,
        )
        return stream + out[None]

    in_specs = (
        P("exp", "tok", "head"),
        P("head", "exp"),
        P("exp", "tok", "head"),
        P(),
        P("exp", "tok", None),
        P("exp", "tok", None),
        P("exp", "tok", None),
        P(("tok", "exp"), "head", None),
        P(("tok", "exp"), "head", None),
        P(("tok", "exp"), "head", None),
    )
    return jax.shard_map(
        on_device, mesh=mesh, in_specs=in_specs, out_specs=P("exp", "tok", "head"), check_vma=False
    )
```

time: 67.6 us -> 62.7 us (0.928)
  Pallas kernels: 65.8 us -> 61.9 us
  other arithmetic: 1.64 us -> 0.67 us
    pallas_call x1, Pallas kernels: 65.8 us -> 61.9 us  [on_device(): pl.pallas_call(functools.partial(kernel, n_tok, n_head, n_exp), out_shape...]
    add x1, other arithmetic: 1.64 us -> 0.67 us  [on_device(): return stream + out[None]]
where the time goes in v2:
time: 62.7 us; the launch traced here: 62.6 us
  Pallas kernels  61.9 us (99%)
  other arithmetic  0.67 us (1%)
    pallas_call x1, Pallas kernels, on_device(): pl.pallas_call(functools.partial(kernel, n_tok, n_head, n_exp), out_shape...  61.9 us

profile of v2, /device:TPU:0, one launch (start us, length us, event | category | flops | bytes accessed | tf_op | source)
XLA Modules:
  0.0 62.6 jit_solution(3140022368494042068)
XLA Ops:
  0.0 0.0 copy-start
  0.0 61.9 %shard_map.100 = f32[32,1024]{1,0:T(8,128)S(1)} custom-call(bf16[32,1024]{1,0:T(8,128)(2,1)} %bitcast.15, bf16[1024,1024]{1,0:T(8,128)(2,1)} %proj_hbm.1, f32[32,1024]{1,0:T(8,128)} %bitcast.14, f32[1,4096]{1,0:T(1,128)} %bitcast.16, s32[8,32]{1,0:T(8,128)} %bitcast.17, s32[8,32]{1,0:T(8,128)} %bitcast.18, f32[8,32]{1,0:T(8,128)} %bitcast.19, ...), custom_call_target="tpu_custom_call" | custom-call | tf_op jit(solution)/shard_map/pallas_call | solution.py:599
  61.9 0.0 copy-done
  61.9 0.7 %bitcast_add_fusion = f32[1,32,1024]{2,1,0:T(8,128)} fusion(f32[1,32,1024]{2,1,0:T(8,128)S(1)} %copy-done, f32[32,1024]{1,0:T(8,128)S(1)} %shard_map.100), kind=kLoop, calls=%fused_computation | loop fusion | flops 32768 | bytes 393216 | tf_op jit(solution)/shard_map/add | solution.py:612
Async XLA Ops:
  0.0 61.9 %copy-start = (f32[1,32,1024]{2,1,0:T(8,128)S(1)}, f32[1,32,1024]{2,1,0:T(8,128)}, u32[]{:S(2)}) copy-start(f32[1,32,1024]{2,1,0:T(8,128)} %param.12) | copy-start | bytes 393220

commit v3 on v2

--- a/solution.py
+++ b/solution.py
@@ -20,11 +20,21 @@
     return [(sum(sizes[:i]), size) for i, size in enumerate(sizes)]
 
 
-def steps_of(width, n_head):
+def batches_of(width, n_head):
+    parts = parts_of(width)
     far, middle = n_head - 1, n_head // 2
-    first = [k for k in range(far - 1, 0, -1)] + [far, 0]
-    rest = [middle] + [k for k in range(far, 0, -1) if k != middle] + [0]
-    return [(k, c) for c in range(len(parts_of(width))) for k in (rest if c else first)]
+    ks = [middle] + [k for k in range(far, 0, -1) if k != middle]
+    first = [(k, 0) for k in range(far - 1, 0, -1)] + [(far, 0)]
+    rest = [(k, c) for c in range(1, len(parts) - 1) for k in ks]
+    rest += [(k, len(parts) - 1) for k in range(far, 0, -1)]
+    own = [(0, c) for c in range(1, len(parts))]
+
+    def cut(steps):
+        n = 1 if parts[steps[0][1]][1] > 256 else 2
+        return [tuple(steps[i : i + n]) for i in range(0, len(steps), n)]
+
+    others = cut(rest)
+    return cut(first) + others[:1] + [((0, 0),)] + others[1:] + cut(own)
 
 
 def partner(a, k):
@@ -38,9 +48,10 @@
 
 def kernel(
     n_tok, n_head, n_exp,
-    ctx_ref, proj_hbm, stream_ref, gain_ref, ids_ref, slots_ref, probs_ref,
+    ctx_hbm, proj_hbm, stream_hbm, gain_hbm, ids_hbm, slots_hbm, probs_hbm,
     wg_hbm, wu_hbm, wd_hbm,
     out_ref,
+    ctx_ref, stream_ref, gain_ref, ids_ref, slots_ref, probs_ref, in_sem,
     proj, wbuf, ctx_all, wall, stream_bf, stream_t, pbf, pown, prs,
     attn_buf, attn_in, ssq, x, gacc, uacc, hid, acc, own, obf, tin, hsend, hrecv, zsend, zrecv,
     fown, fzsend, fzrecv, fsend, frecv,
@@ -53,6 +64,15 @@
     n_local, n_hid, model = wg_hbm.shape
     depth = ctx_ref.shape[1]
     tokens = n_tok * n_exp * rows
+    inputs = [
+        pltpu.make_async_copy(source, target, in_sem.at[n])
+        for n, (source, target) in enumerate((
+            (ctx_hbm, ctx_ref), (stream_hbm, stream_ref), (ids_hbm, ids_ref),
+            (slots_hbm, slots_ref), (probs_hbm, probs_ref), (gain_hbm, gain_ref),
+        ))
+    ]
+    for c in inputs:
+        c.start()
     parts = parts_of(width)
     turned = {"tok": t, "head": e, "exp": h}
     mine = h == e
@@ -78,12 +98,20 @@
     on_head = [{"head": i} for i in head_of]
     on_tok = {"tok": 1 - t}
 
+    barrier = pltpu.get_barrier_semaphore()
+    for device in on_exp[1:] + on_head[1:] + [on_tok]:
+        pl.semaphore_signal(barrier, inc=1, device_id=device, device_id_type=MESH)
+
+    @pl.when(jnp.logical_not(mine))
+    def _():
+        pl.semaphore_signal(barrier, inc=1, device_id=turned, device_id_type=MESH)
+
     def lanes(i, size):
         return pl.ds(pl.multiple_of(i * size, min(size, LANES)), size)
 
     n_part = max(1, n_local - 1)
-    steps = steps_of(width, n_head)
-    n_steps = len(steps)
+    batches = batches_of(width, n_head)
+    steps = [step for batch in batches for step in batch]
     proj_c = pltpu.make_async_copy(proj_hbm, proj, proj_sem)
     proj_c.start()
 
@@ -132,19 +160,13 @@
                 for i in range(n_exp):
                     if late(j, m, i)[2] == p:
                         late_copy(j, m, i).start()
-        for s in range(n_steps):
+        for s in range(len(steps)):
             for j in range(n_local):
                 if down(s, j)[2] == p:
                     d_copy(s, j).start()
 
-    barrier = pltpu.get_barrier_semaphore()
-    for device in on_exp[1:] + on_head[1:] + [on_tok]:
-        pl.semaphore_signal(barrier, inc=1, device_id=device, device_id_type=MESH)
-
-    @pl.when(jnp.logical_not(mine))
-    def _():
-        pl.semaphore_signal(barrier, inc=1, device_id=turned, device_id_type=MESH)
-
+    for c in inputs:
+        c.wait()
     stream_bf[...] = stream_ref[...].astype(BF16)
     lane = lax.broadcasted_iota(jnp.int32, (rows, LANES), 1)
     n_experts = wall.shape[2]
@@ -192,6 +214,12 @@
                 ctx_c[j].wait_recv()
             pieces.append(ctx_all[exp_of[j]] if j else ctx_ref[...])
         pieces = jnp.concatenate(pieces, axis=0)
+        if group[-1] == order[-1]:
+
+            @pl.when(jnp.logical_not(mine))
+            def _():
+                stream_c.start()
+
 
         def project(i, carry):
             cols = lanes(i, tile)
@@ -212,12 +240,6 @@
             @pl.when(exp_of[j] != h)
             def _():
                 prs_c(j).start()
-
-        if group == order[:1]:
-
-            @pl.when(jnp.logical_not(mine))
-            def _():
-                stream_c.start()
 
     arrived(prs.at[pl.ds(0, n_head - 1)], prs_r)
     attn = pown[...]
@@ -326,16 +348,15 @@
         number = (t * n_exp + e) * n_local + j
         expert_of = lax.broadcasted_iota(jnp.int32, wall.shape, 2)
         picked = jnp.where(expert_of == number, wall[...], 0.0)
-        return scale, column(jnp.sum(picked, axis=2, keepdims=True))
-
-    def finish(j, i, g, u, scale, gate_w):
+        return 0.5 * scale, scale * column(jnp.sum(picked, axis=2, keepdims=True))
+
+    def finish(j, i, g, u, scale, factor):
         g = g * scale
-        u = u * scale
-        hid[j, :, lanes(i, hid_tile)] = (g / (1.0 + jnp.exp(-g)) * u * gate_w).astype(BF16)
+        hid[j, :, lanes(i, hid_tile)] = ((g + g * jnp.tanh(g)) * (u * factor)).astype(BF16)
 
     def up_part(j, p):
         cols = lanes(exp_of[p], width)
-        scale, gate_w = factors(j) if p == n_exp - 1 else (None, None)
+        scale, factor = factors(j) if p == n_exp - 1 else (None, None)
 
         def body(i, carry):
             q = j * n_tiles + i
@@ -350,13 +371,13 @@
                 gacc[q] = g
                 uacc[q] = u
             else:
-                finish(j, i, g, u, scale, gate_w)
+                finish(j, i, g, u, scale, factor)
             return carry
 
         lax.fori_loop(0, n_tiles, body, 0, unroll=True)
 
     def up_whole(j):
-        scale, gate_w = factors(j)
+        scale, factor = factors(j)
 
         def body(i, carry):
             span = lanes(i, hid_tile)
@@ -370,7 +391,7 @@
                         wbuf[slot, span, cols], dims, preferred_element_type=F32,
                     )
                 both.append(value)
-            finish(j, i, both[0], both[1], scale, gate_w)
+            finish(j, i, both[0], both[1], scale, factor)
             return carry
 
         lax.fori_loop(0, n_tiles, body, 0, unroll=True)
@@ -384,11 +405,10 @@
             if p == 0:
                 loaded(wbuf.at[pl.ds(0, 2)], w_sem.at[j])
             up_part(j, p)
-            if j == 0:
+            if j == max(0, n_part - 2):
                 forward(p + 3)
+                share(p + 1)
                 small(p)
-            if j == max(0, n_part - 2):
-                share(p + 1)
         load_after(p)
     for j in range(n_part, n_local):
         loaded(wbuf.at[pl.ds(0, 2)], l_sem.at[j - n_part])
@@ -481,19 +501,20 @@
             obf[c][k] = value[1].astype(BF16)
             to_c[s].start()
 
-    batches, s = [], 0
-    while s < n_steps:
-        n = 1 if parts[steps[s][1]][1] > 256 else 2
-        batches.append(range(s, s + n))
-        s += n
+    done, s = [], 0
     for b, batch in enumerate(batches):
-        down_steps(batch)
-        for s in batches[b - 1] if b else ():
-            head_step(s)
-        if len(parts) > 2 and batch[-1] == 2 * n_head + 1:
+        down_steps(range(s, s + len(batch)))
+        for n in done:
+            head_step(n)
+        done = range(s, s + len(batch))
+        s += len(batch)
+        if len(parts) > 2 and b == len(batches) - 2:
             exp_step(0)
-    for s in batches[-1]:
-        head_step(s)
+            for n in done:
+                head_step(n)
+            done = ()
+    for n in done:
+        head_step(n)
     some = pl.ds(0, n_exp - 1)
     sent(ctx_all.at[some], ctx_s)
     sent(pbf.at[some], prs_s)
@@ -549,16 +570,23 @@
         depth = context.shape[2]
         parts = parts_of(width)
         n_parts = len(parts)
-        n_steps = len(steps_of(width, n_head))
+        n_steps = sum(len(batch) for batch in batches_of(width, n_head))
         hid_tile = 256 if n_hid % 256 == 0 else n_hid
         n_tiles = n_hid // hid_tile
         n_part = max(1, n_local - 1)
         vmem = pl.BlockSpec(memory_space=pltpu.VMEM)
-        hbm = pl.BlockSpec(memory_space=pl.ANY)
+        hbm = pl.BlockSpec(memory_space=pltpu.HBM)
         dma = pltpu.SemaphoreType.DMA
         V = pltpu.VMEM
         n_slots = max(2 * n_part, 3 * n_local - 2 * n_part)
         scratch = [
+            V(context.shape[1:], BF16),
+            V((rows, width), F32),
+            V((1, model), F32),
+            V((expert_ids.shape[2], rows), jnp.int32),
+            V((expert_ids.shape[2], rows), jnp.int32),
+            V((expert_ids.shape[2], rows), F32),
+            dma((6,)),
             V(out_proj.shape, BF16),
             V((n_slots, n_hid, model), BF16),
             V((n_exp, rows, depth), BF16),
@@ -599,7 +627,7 @@
         out = pl.pallas_call(
             functools.partial(kernel, n_tok, n_head, n_exp),
             out_shape=pltpu.VMEM((rows, width), F32),
-            in_specs=[vmem, hbm, vmem, vmem, vmem, vmem, vmem, hbm, hbm, hbm],
+            in_specs=[hbm] * 10,
             out_specs=vmem,
             scratch_shapes=scratch,
             compiler_params=pltpu.CompilerParams(

time: 62.7 us -> 61.8 us (0.986)
  Pallas kernels: 61.9 us -> 61 us
    pallas_call x1, Pallas kernels: 61.9 us -> 61 us  [on_device(): pl.pallas_call(functools.partial(kernel, n_tok, n_head, n_exp), out_shape...]
where the time goes in v3:
time: 61.8 us; the launch traced here: 61.7 us
  Pallas kernels  61 us (99%)
  other arithmetic  0.67 us (1%)
    pallas_call x1, Pallas kernels, on_device(): pl.pallas_call(functools.partial(kernel, n_tok, n_head, n_exp), out_shape...  61 us

profile of v3, /device:TPU:0, one launch (start us, length us, event | category | flops | bytes accessed | tf_op | source)
XLA Modules:
  0.0 61.7 jit_solution(12621605433248072347)
XLA Ops:
  0.0 0.0 copy-start
  0.0 61.0 %shard_map.100 = f32[32,1024]{1,0:T(8,128)S(1)} custom-call(bf16[32,1024]{1,0:T(8,128)(2,1)} %bitcast.15, bf16[1024,1024]{1,0:T(8,128)(2,1)} %proj_hbm.1, f32[32,1024]{1,0:T(8,128)} %bitcast.14, f32[1,4096]{1,0:T(1,128)} %bitcast.16, s32[8,32]{1,0:T(8,128)} %bitcast.17, s32[8,32]{1,0:T(8,128)} %bitcast.18, f32[8,32]{1,0:T(8,128)} %bitcast.19, ...), custom_call_target="tpu_custom_call" | custom-call | tf_op jit(solution)/shard_map/pallas_call | solution.py:627
  61.0 0.0 copy-done
  61.0 0.7 %bitcast_add_fusion = f32[1,32,1024]{2,1,0:T(8,128)} fusion(f32[1,32,1024]{2,1,0:T(8,128)S(1)} %copy-done, f32[32,1024]{1,0:T(8,128)S(1)} %shard_map.100), kind=kLoop, calls=%fused_computation | loop fusion | flops 32768 | bytes 393216 | tf_op jit(solution)/shard_map/add | solution.py:640
Async XLA Ops:
  0.0 61.0 %copy-start = (f32[1,32,1024]{2,1,0:T(8,128)S(1)}, f32[1,32,1024]{2,1,0:T(8,128)}, u32[]{:S(2)}) copy-start(f32[1,32,1024]{2,1,0:T(8,128)} %param.12) | copy-start | bytes 393220

commit v4 on v3

--- a/solution.py
+++ b/solution.py
@@ -22,9 +22,9 @@
 
 def batches_of(width, n_head):
     parts = parts_of(width)
-    far, middle = n_head - 1, n_head // 2
-    ks = [middle] + [k for k in range(far, 0, -1) if k != middle]
-    first = [(k, 0) for k in range(far - 1, 0, -1)] + [(far, 0)]
+    far = n_head - 1
+    ks = list(range(far - 1, 0, -1)) + [far]
+    first = [(k, 0) for k in ks]
     rest = [(k, c) for c in range(1, len(parts) - 1) for k in ks]
     rest += [(k, len(parts) - 1) for k in range(far, 0, -1)]
     own = [(0, c) for c in range(1, len(parts))]
@@ -34,7 +34,7 @@
         return [tuple(steps[i : i + n]) for i in range(0, len(steps), n)]
 
     others = cut(rest)
-    return cut(first) + others[:1] + [((0, 0),)] + others[1:] + cut(own)
+    return cut(first) + others[:-1] + [((0, 0),)] + others[-1:] + cut(own)
 
 
 def partner(a, k):
@@ -414,7 +414,7 @@
         loaded(wbuf.at[pl.ds(0, 2)], l_sem.at[j - n_part])
         up_whole(j)
 
-    far = n_head - 1
+    far, n_first = n_head - 1, len(fown)
     to_c = [
         send(obf[c].at[k], tin[c].at[k], to_s.at[c], to_r.at[k, c], on_tok) for k, c in steps
     ]
@@ -423,7 +423,7 @@
     first_of = (near, (n_exp - group) - near)
 
     def heads_of(c):
-        return range(1, n_head) if c else range(1, far)
+        return range(1, far) if c < n_first else range(1, n_head)
 
     def ho_c(k, c, g):
         at = (k - 1, pl.ds(first_of[g], group))
@@ -437,24 +437,25 @@
     def heads_arrived(c, g):
         arrived(hrecv[c].at[pl.ds(0, len(heads_of(c))), pl.ds(0, group)], ho_r.at[c, g])
 
-    fz_c = [
-        send(fzsend.at[m - 1], fzrecv.at[m - 1], fz_s, fz_r, on_exp[m])
-        for m in range(1, n_exp)
+    def fz_c(m, c):
+        return send(fzsend[c].at[m - 1], fzrecv[c].at[m - 1], fz_s.at[c], fz_r.at[c], on_exp[m])
+
+    fh_c = [
+        send(fsend[c], frecv[c], fh_s.at[c], fh_r.at[c], on_head[far]) for c in range(n_first)
     ]
-    fh_c = send(fsend, frecv, fh_s, fh_r, on_head[far])
 
     def head_step(s):
         k, c = steps[s]
         to_c[s].wait_recv()
-        if k == far and c == 0:
+        if k == far and c < n_first:
             for m in range(n_exp - 1, -1, -1):
                 i = exp_of[m]
                 value = acc[c][s % 4, i] + tin[c][k, i].astype(F32)
                 if m:
-                    fzsend[m - 1] = value.astype(BF16)
-                    fz_c[m - 1].start()
+                    fzsend[c][m - 1] = value.astype(BF16)
+                    fz_c(m, c).start()
                 else:
-                    fown[...] = value
+                    fown[c][...] = value
         elif k:
             hsend[c][k - 1] = (acc[c][s % 4] + tin[c][k].astype(F32)).astype(BF16)
             for g in (1, 0):
@@ -462,13 +463,13 @@
         else:
             own[c][...] = acc[c][s % 4] + tin[c][k].astype(F32)
 
-    def far_step():
-        value = fown[...]
-        arrived(fzrecv, fz_r)
+    def far_step(c):
+        value = fown[c][...]
+        arrived(fzrecv[c], fz_r.at[c])
         for m in range(n_exp - 1, 0, -1):
-            value = value + fzrecv[m - 1].astype(F32)
-        fsend[...] = value.astype(BF16)
-        fh_c.start()
+            value = value + fzrecv[c][m - 1].astype(F32)
+        fsend[c][...] = value.astype(BF16)
+        fh_c[c].start()
 
     def summed(m, c):
         value = own[c][exp_of[m]]
@@ -476,10 +477,9 @@
             value = value + hrecv[c][k - 1, exp_of[m]].astype(F32)
         return value
 
-    def exp_step(c):
-        for m in range(n_exp - 1, 0, -1):
-            if m in (n_exp - 1, group - 1):
-                heads_arrived(c, m // group)
+    def exp_step(c, g):
+        heads_arrived(c, g)
+        for m in range((g + 1) * group - 1, max(g * group, 1) - 1, -1):
             zsend[c][m - 1] = summed(m, c).astype(BF16)
             zo_c(m, c).start()
 
@@ -509,10 +509,12 @@
         done = range(s, s + len(batch))
         s += len(batch)
         if len(parts) > 2 and b == len(batches) - 2:
-            exp_step(0)
+            exp_step(0, 1)
             for n in done:
                 head_step(n)
             done = ()
+        if len(parts) > 2 and b == len(batches) - 1:
+            exp_step(0, 0)
     for n in done:
         head_step(n)
     some = pl.ds(0, n_exp - 1)
@@ -526,9 +528,14 @@
     sent(wall.at[0, some], wz_s)
     wt_c.wait_send()
     qt_c.wait_send()
-    far_step()
-    for c in range(1 if len(parts) > 2 else 0, len(parts)):
-        exp_step(c)
+    left = range(1 if len(parts) > 2 else 0, len(parts))
+    exp_step(left[0], 1)
+    for c in range(n_first):
+        far_step(c)
+    exp_step(left[0], 0)
+    for c in left[1:]:
+        exp_step(c, 1)
+        exp_step(c, 0)
 
     @pl.when(jnp.logical_not(mine))
     def _():
@@ -539,12 +546,10 @@
         attn_in[...] = attn_buf[...]
 
     for c, (first, size) in enumerate(parts):
-        if group == 1:
-            heads_arrived(c, 0)
         value = summed(0, c) + attn_in[:, first : first + size]
-        if c == 0:
-            fh_c.wait_recv()
-            value = value + frecv[...].astype(F32)
+        if c < n_first:
+            fh_c[c].wait_recv()
+            value = value + frecv[c][...].astype(F32)
         arrived(zrecv[c], zo_r.at[c])
         for m in range(n_exp - 1, 0, -1):
             value = value + zrecv[c][m - 1].astype(F32)
@@ -554,8 +559,9 @@
         sent(obf[c], to_s.at[c])
         sent(hsend[c].at[pl.ds(0, len(heads_of(c)))], ho_s.at[c])
         sent(zsend[c], zo_s.at[c])
-    sent(fzsend, fz_s)
-    fh_c.wait_send()
+    for c in range(n_first):
+        sent(fzsend[c], fz_s.at[c])
+        fh_c[c].wait_send()
 
 
 def solution(mesh):
@@ -611,18 +617,19 @@
             [V((n_head - 1, n_exp, rows, size), BF16) for _, size in parts],
             [V((n_exp - 1, rows, size), BF16) for _, size in parts],
             [V((n_exp - 1, rows, size), BF16) for _, size in parts],
-            V((rows, parts[0][1]), F32),
-            V((n_exp - 1, rows, parts[0][1]), BF16),
-            V((n_exp - 1, rows, parts[0][1]), BF16),
-            V((rows, parts[0][1]), BF16),
-            V((rows, parts[0][1]), BF16),
+            [V((rows, size), F32) for _, size in parts[:-1]],
+            [V((n_exp - 1, rows, size), BF16) for _, size in parts[:-1]],
+            [V((n_exp - 1, rows, size), BF16) for _, size in parts[:-1]],
+            [V((rows, size), BF16) for _, size in parts[:-1]],
+            [V((rows, size), BF16) for _, size in parts[:-1]],
             dma, dma((n_part,)), dma((max(1, n_local - n_part),)), dma((n_steps,)),
             dma, dma((n_exp,)), dma, dma, dma, dma, dma, dma,
             dma, dma, dma, dma,
             dma, dma((n_exp,)), dma, dma, dma, dma((n_head - 1, n_exp)), dma, dma,
             dma, dma((n_exp,)), dma, dma,
             dma((n_parts,)), dma((n_head, n_parts)), dma((n_parts,)), dma((n_parts, 2)),
-            dma((n_parts,)), dma((n_parts,)), dma, dma, dma, dma,
+            dma((n_parts,)), dma((n_parts,)),
+            dma((n_parts - 1,)), dma((n_parts - 1,)), dma((n_parts - 1,)), dma((n_parts - 1,)),
         ]
         out = pl.pallas_call(
             functools.partial(kernel, n_tok, n_head, n_exp),

time: 61.8 us -> 60.3 us (0.976)
  Pallas kernels: 61 us -> 59.5 us
    pallas_call x1, Pallas kernels: 61 us -> 59.5 us  [on_device(): pl.pallas_call(functools.partial(kernel, n_tok, n_head, n_exp), out_shape...]
where the time goes in v4:
time: 60.3 us; the launch traced here: 60.2 us
  Pallas kernels  59.5 us (99%)
  other arithmetic  0.67 us (1%)
    pallas_call x1, Pallas kernels, on_device(): pl.pallas_call(functools.partial(kernel, n_tok, n_head, n_exp), out_shape...  59.5 us

profile of v4, /device:TPU:0, one launch (start us, length us, event | category | flops | bytes accessed | tf_op | source)
XLA Modules:
  0.0 60.2 jit_solution(16151006352802546305)
XLA Ops:
  0.0 0.0 copy-start
  0.0 59.5 %shard_map.100 = f32[32,1024]{1,0:T(8,128)S(1)} custom-call(bf16[32,1024]{1,0:T(8,128)(2,1)} %bitcast.15, bf16[1024,1024]{1,0:T(8,128)(2,1)} %proj_hbm.1, f32[32,1024]{1,0:T(8,128)} %bitcast.14, f32[1,4096]{1,0:T(1,128)} %bitcast.16, s32[8,32]{1,0:T(8,128)} %bitcast.17, s32[8,32]{1,0:T(8,128)} %bitcast.18, f32[8,32]{1,0:T(8,128)} %bitcast.19, ...), custom_call_target="tpu_custom_call" | custom-call | tf_op jit(solution)/shard_map/pallas_call | solution.py:634
  59.5 0.0 copy-done
  59.5 0.7 %bitcast_add_fusion = f32[1,32,1024]{2,1,0:T(8,128)} fusion(f32[1,32,1024]{2,1,0:T(8,128)S(1)} %copy-done, f32[32,1024]{1,0:T(8,128)S(1)} %shard_map.100), kind=kLoop, calls=%fused_computation | loop fusion | flops 32768 | bytes 393216 | tf_op jit(solution)/shard_map/add | solution.py:647
Async XLA Ops:
  0.0 59.5 %copy-start = (f32[1,32,1024]{2,1,0:T(8,128)S(1)}, f32[1,32,1024]{2,1,0:T(8,128)}, u32[]{:S(2)}) copy-start(f32[1,32,1024]{2,1,0:T(8,128)} %param.12) | copy-start | bytes 393220

commit v5 on v4

--- a/solution.py
+++ b/solution.py
@@ -12,7 +12,7 @@
 F32 = jnp.float32
 BF16 = jnp.bfloat16
 eps_value = 1e-05
-VMEM_BYTES = 62_500_000
+VMEM_BYTES = 63_000_000
 
 
 def parts_of(width):
@@ -225,13 +225,9 @@
             cols = lanes(i, tile)
             part = jnp.dot(pieces, proj[:, cols], preferred_element_type=F32)
             for n, j in enumerate(group):
-                mine_part = part[n * rows : (n + 1) * rows]
-                pbf[exp_of[j], :, cols] = mine_part.astype(BF16)
-
-                @pl.when(exp_of[j] == h)
-                def _():
-                    pown[:, cols] = mine_part
-
+                piece = part[n * rows : (n + 1) * rows]
+                pbf[exp_of[j], :, cols] = piece.astype(BF16)
+                pown[exp_of[j], :, cols] = piece
             return carry
 
         lax.fori_loop(0, width // tile, project, 0, unroll=True)
@@ -242,7 +238,7 @@
                 prs_c(j).start()
 
     arrived(prs.at[pl.ds(0, n_head - 1)], prs_r)
-    attn = pown[...]
+    attn = pown[h]
     for k in range(1, n_head):
         attn = attn + prs[head_of[k]].astype(F32)
     attn_buf[...] = attn
@@ -260,11 +256,6 @@
     own_cols = lanes(e, width)
     resid = attn + stream_t[...].astype(F32)
     x[0, h, :, own_cols] = (resid * gain_ref[:, own_cols]).astype(BF16)
-    square = jnp.sum(resid * resid, axis=1, keepdims=True)
-    row_id = lax.broadcasted_iota(jnp.int32, (rows, LANES), 0)
-    flat = jnp.sum(jnp.where(row_id == lane, square, 0.0), axis=0, keepdims=True)
-    ssq[0, h, e] = jnp.broadcast_to(flat, (8, LANES))
-
     def x_at(s, k, j):
         return x.at[s, head_of[k], :, lanes(exp_of[j], width)]
 
@@ -325,6 +316,10 @@
     forward(0)
     for j in range(1, n_exp):
         xz_c[j].start()
+    square = jnp.sum(resid * resid, axis=1, keepdims=True)
+    row_id = lax.broadcasted_iota(jnp.int32, (rows, LANES), 0)
+    flat = jnp.sum(jnp.where(row_id == lane, square, 0.0), axis=0, keepdims=True)
+    ssq[0, h, e] = jnp.broadcast_to(flat, (8, LANES))
     for c in qz_c:
         c.start()
     forward(1)
@@ -600,7 +595,7 @@
             V((rows, width), BF16),
             V((rows, width), BF16),
             V((n_exp, rows, width), BF16),
-            V((rows, width), F32),
+            V((n_exp, rows, width), F32),
             V((n_head, rows, width), BF16),
             V((rows, width), F32),
             V((rows, width), F32),

time: 60.3 us -> 59.8 us (level)
  no operation moved by 1% of the time
where the time goes in v5:
time: 59.8 us; the launch traced here: 59.6 us
  Pallas kernels  58.9 us (98%)
  other arithmetic  0.67 us (1%)
    pallas_call x1, Pallas kernels, on_device(): pl.pallas_call(functools.partial(kernel, n_tok, n_head, n_exp), out_shape...  58.9 us

profile of v5, /device:TPU:0, one launch (start us, length us, event | category | flops | bytes accessed | tf_op | source)
XLA Modules:
  0.0 59.6 jit_solution(17005066544609468168)
XLA Ops:
  0.0 0.0 copy-start
  0.0 58.9 %shard_map.100 = f32[32,1024]{1,0:T(8,128)S(1)} custom-call(bf16[32,1024]{1,0:T(8,128)(2,1)} %bitcast.15, bf16[1024,1024]{1,0:T(8,128)(2,1)} %proj_hbm.1, f32[32,1024]{1,0:T(8,128)} %bitcast.14, f32[1,4096]{1,0:T(1,128)} %bitcast.16, s32[8,32]{1,0:T(8,128)} %bitcast.17, s32[8,32]{1,0:T(8,128)} %bitcast.18, f32[8,32]{1,0:T(8,128)} %bitcast.19, ...), custom_call_target="tpu_custom_call" | custom-call | tf_op jit(solution)/shard_map/pallas_call | solution.py:629
  58.9 0.0 copy-done
  59.0 0.7 %bitcast_add_fusion = f32[1,32,1024]{2,1,0:T(8,128)} fusion(f32[1,32,1024]{2,1,0:T(8,128)S(1)} %copy-done, f32[32,1024]{1,0:T(8,128)S(1)} %shard_map.100), kind=kLoop, calls=%fused_computation | loop fusion | flops 32768 | bytes 393216 | tf_op jit(solution)/shard_map/add | solution.py:642
Async XLA Ops:
  0.0 58.9 %copy-start = (f32[1,32,1024]{2,1,0:T(8,128)S(1)}, f32[1,32,1024]{2,1,0:T(8,128)}, u32[]{:S(2)}) copy-start(f32[1,32,1024]{2,1,0:T(8,128)} %param.12) | copy-start | bytes 393220
